TPU v7x, 512 devices: a whole 4x8x8 slice. The times are simulated.
512 devices in a mesh: gx: 16 (over z, core), gy: 8 (over y), gz: 4 (over x).
Axes of the slice: x: 4, y: 8, z: 8, core: 2. Of those that a mesh axis runs over, the one named last changes fastest.
Arguments:
- snapshot: float32 [512, 1280, 512], P('gx', 'gy', 'gz'), may hold values from -40 to 40
Outputs:
- basis: float32 [512, 128], P('gx')
- core: float32 [128, 1280, 512], P('gx', 'gy', 'gz')
All inputs are finite; a program needn't handle non-finite values.
Results may differ from a plain program's by a relative error of at most 0.0002.
Values sent between devices are 32-bit elements; how exact they have to be, the bound alone decides.
A program may use at most 64 MiB of HBM per device.

v0:
```python
import jax
import jax.numpy as jnp
from jax import lax
from jax.sharding import PartitionSpec as P

RANK = 128
ITERS = 2


def product(left, right):
    return jnp.dot(left, right, precision=lax.Precision.HIGHEST, preferred_element_type=jnp.float32)


def orthonormal(matrix):
    lower = jnp.linalg.cholesky(product(matrix.T, matrix))
    return jax.scipy.linalg.solve_triangular(lower, matrix.T, lower=True).T


def local(snapshot):
    xlocal, ylocal, zlocal = snapshot.shape
    flat = snapshot.reshape(xlocal, ylocal * zlocal)
    fibres = lax.all_to_all(flat, "gx", split_axis=1, concat_axis=0, tiled=True)
    gram = product(fibres, fibres.T)
    factor = jnp.linalg.cholesky(lax.psum(gram, ("gx", "gy", "gz")))
    basis = orthonormal(factor[:, :RANK])
    for step in range(ITERS):
        basis = orthonormal(product(factor, product(factor.T, basis)))
    groups = lax.axis_size("gx")
    own_rows = basis.shape[0] // groups
    mine = lax.dynamic_slice_in_dim(basis, lax.axis_index("gx") * own_rows, own_rows, 0)
    projected = product(basis.T, fibres)
    returned = lax.all_to_all(projected, "gx", split_axis=0, concat_axis=1, tiled=True)
    return (mine, returned.reshape(RANK // groups, ylocal, zlocal))


def solution(mesh):
    in_specs = (P("gx", "gy", "gz"),)
    out_specs = (P("gx", None), P("gx", "gy", "gz"))
    return jax.shard_map(local, mesh=mesh, in_specs=in_specs, out_specs=out_specs, check_vma=False)
```

profile of v0, /device:TPU:1, one launch (start us, length us, event | category | flops | bytes accessed | tf_op | source)
XLA Modules:
  0.0 580.8 jit_solution(15275635226569136335)
XLA Ops:
  7.2 2.6 all_to_all.24
  9.8 1.5 copy.10
  11.3 73.8 %all_to_all.32 = f32[32,16,1280]{2,0,1:T(8,128)S(1)} all-to-all(f32[32,16,1280]{2,0,1:T(8,128)S(1)} %copy.10), channel_id=1, replica_groups=mesh['gx'=16,'gy'=8,'gz'=4] {'gx'}, dimensions={1} | all-to-all | bytes 5242880 | tf_op jit(solution)/shard_map/all_to_all | solution.py:22
  85.1 5.3 fusion.50
  90.5 272.2 %all-reduce.3.cloned.1.call-done = f32[512,512]{0,1:T(8,128)} async-done(((f32[512,512]{0,1:T(8,128)}), f32[512,512]{0,1:T(8,128)}) %all-reduce.3.cloned.1.call-update) | async-done | bytes 1048592 | tf_op jit(solution)/shard_map/psum | solution.py:24
  362.7 2.6 copy.12
  365.3 1.8 fusion
  368.1 11.7 %cholesky.120 = f32[128,128]{1,0:T(8,128)S(1)} custom-call(f32[128,128]{1,0:T(8,128)S(1)} %cholesky.356), custom_call_target="Cholesky" | custom-call | tf_op jit(solution)/shard_map/jit(cholesky)/cholesky | solution.py:24
  379.8 9.8 %custom-call.32 = f32[1,128,128]{1,2,0:T(8,128)S(1)} custom-call(f32[1,128,128]{2,1,0:T(8,128)S(1)} %get-tuple-element.17), custom_call_target="InvertDiagBlocksLowerTriangular" | custom-call | tf_op jit(solution)/shard_map/jit(cholesky)/cholesky | solution.py:24
  389.6 1.2 cholesky.251
  390.8 2.0 constant_dynamic-update-slice_fusion.2
  392.8 1.3 convolution_subtract_fusion
  394.0 11.9 %cholesky.244 = f32[128,128]{1,0:T(8,128)S(1)} custom-call(f32[128,128]{1,0:T(8,128)S(1)} %cholesky.360), custom_call_target="Cholesky" | custom-call | tf_op jit(solution)/shard_map/jit(cholesky)/cholesky | solution.py:24
  406.5 9.8 %custom-call.33 = f32[1,128,128]{1,2,0:T(8,128)S(1)} custom-call(f32[1,128,128]{2,1,0:T(8,128)S(1)} %get-tuple-element.14), custom_call_target="InvertDiagBlocksLowerTriangular" | custom-call | tf_op jit(solution)/shard_map/jit(cholesky)/cholesky | solution.py:24
  417.3 1.4 convolution_subtract_fusion.1
  418.7 11.7 %cholesky.265 = f32[128,128]{1,0:T(8,128)S(1)} custom-call(f32[128,128]{1,0:T(8,128)S(1)} %cholesky.365), custom_call_target="Cholesky" | custom-call | tf_op jit(solution)/shard_map/jit(cholesky)/cholesky | solution.py:24
  431.7 10.0 %custom-call.34 = f32[1,128,128]{1,2,0:T(8,128)S(1)} custom-call(f32[1,128,128]{2,1,0:T(8,128)S(1)} %get-tuple-element.11), custom_call_target="InvertDiagBlocksLowerTriangular" | custom-call | tf_op jit(solution)/shard_map/jit(cholesky)/cholesky | solution.py:24
  442.6 1.4 convolution_subtract_fusion.2
  444.0 11.7 %cholesky.282 = f32[128,128]{1,0:T(8,128)S(1)} custom-call(f32[128,128]{1,0:T(8,128)S(1)} %convolution_subtract_fusion.2), custom_call_target="Cholesky" | custom-call | tf_op jit(solution)/shard_map/jit(cholesky)/cholesky | solution.py:24
  460.3 1.4 select_select_fusion
  463.4 11.7 %cholesky.325 = f32[128,128]{1,0:T(8,128)S(1)} custom-call(f32[128,128]{1,0:T(8,128)S(1)} %fusion.28), custom_call_target="Cholesky" | custom-call | tf_op jit(solution)/shard_map/jit(cholesky)/cholesky | solution.py:15
  476.4 9.8 %custom-call.37 = f32[1,128,128]{1,2,0:T(8,128)S(1)} custom-call(f32[1,128,128]{2,1,0:T(8,128)S(1)} %fusion.18), custom_call_target="InvertDiagBlocksLowerTriangular" | custom-call | tf_op jit(solution)/shard_map/jit(_solve_triangular)/triangular_solve | solution.py:16
  486.2 1.5 fusion.8
  487.7 3.4 fusion.51
  492.9 11.7 %cholesky.336 = f32[128,128]{1,0:T(8,128)S(1)} custom-call(f32[128,128]{1,0:T(8,128)S(1)} %fusion.26), custom_call_target="Cholesky" | custom-call | tf_op jit(solution)/shard_map/jit(cholesky)/cholesky | solution.py:15
  505.9 9.8 %custom-call.38 = f32[1,128,128]{1,2,0:T(8,128)S(1)} custom-call(f32[1,128,128]{2,1,0:T(8,128)S(1)} %fusion.19), custom_call_target="InvertDiagBlocksLowerTriangular" | custom-call | tf_op jit(solution)/shard_map/jit(_solve_triangular)/triangular_solve | solution.py:16
  516.2 3.0 fusion.54
  521.1 11.7 %cholesky.347 = f32[128,128]{1,0:T(8,128)S(1)} custom-call(f32[128,128]{1,0:T(8,128)S(1)} %fusion.24), custom_call_target="Cholesky" | custom-call | tf_op jit(solution)/shard_map/jit(cholesky)/cholesky | solution.py:15
  534.1 9.8 %custom-call.39 = f32[1,128,128]{1,2,0:T(8,128)S(1)} custom-call(f32[1,128,128]{2,1,0:T(8,128)S(1)} %fusion.20), custom_call_target="InvertDiagBlocksLowerTriangular" | custom-call | tf_op jit(solution)/shard_map/jit(_solve_triangular)/triangular_solve | solution.py:16
  544.4 2.3 fusion.2
  546.7 6.0 %all-to-all-start.1 = ((f32[16,8,1280]{2,1,0:T(8,128)}), f32[16,8,1280]{2,1,0:T(8,128)S(1)}, u32[]{:S(2)}, u32[]{:S(2)}) async-start(f32[16,8,1280]{2,1,0:T(8,128)} %fusion.2), calls=%async_computation.1 | async-start | bytes 1310720 | tf_op jit(solution)/shard_map/all_to_all | solution.py:32
  553.5 19.2 %all-to-all-done.1 = f32[16,8,1280]{2,1,0:T(8,128)S(1)} async-done(((f32[16,8,1280]{2,1,0:T(8,128)}), f32[16,8,1280]{2,1,0:T(8,128)S(1)}, u32[]{:S(2)}, u32[]{:S(2)}) %all-to-all-start.1) | async-done | bytes 655392 | tf_op jit(solution)/shard_map/all_to_all | solution.py:32
  (48 shorter events, 18.7 us)
Async XLA Ops:
  7.2 355.5 %all-reduce.3.cloned.1.call-start = ((), (), s32[]{:S(2)}) async-start(), calls=%async_computation.2 | async-start | bytes 2097152 | tf_op jit(solution)/shard_map/psum | solution.py:24
  367.1 1.0 copy-start.3
  461.7 1.0 copy-start
  486.2 4.9 copy-start.1
  515.7 3.5 copy-start.2
  546.7 26.0 %all-to-all-start.1 = ((f32[16,8,1280]{2,1,0:T(8,128)}), f32[16,8,1280]{2,1,0:T(8,128)S(1)}, u32[]{:S(2)}, u32[]{:S(2)}) async-start(f32[16,8,1280]{2,1,0:T(8,128)} %fusion.2), calls=%async_computation.1 | async-start | bytes 1310720 | tf_op jit(solution)/shard_map/all_to_all | solution.py:32
Sparse Core Ops, SparseCore 0:
  90.6 272.0 all-reduce.2
where the time goes:
time: 584 us; the launch traced here: 581 us
  waiting for transfers between devices  291 us (50%)
  other arithmetic  152 us (26%)
  blocking collectives  73.8 us (13%)
  matrix products  28.1 us (5%)
  between operations  17.1 us (3%)
  local copies, waits for them, and re-layouts  12 us (2%)
  starting transfers between devices  6.06 us (1%)
    psum x1, waiting for transfers between devices, local(): factor = jnp.linalg.cholesky(lax.psum(gram, ('gx', 'gy', 'gz')))  272 us
    another operation x14, other arithmetic, local(): factor = jnp.linalg.cholesky(lax.psum(gram, ('gx', 'gy', 'gz')))  80.6 us
    all_to_all x1, blocking collectives, local(): fibres = lax.all_to_all(flat, 'gx', split_axis=1, concat_axis=0, tiled=True)  73.8 us
    another operation x9, other arithmetic, orthonormal(): lower = jnp.linalg.cholesky(product(matrix.T, matrix))  37.2 us
    another operation x6, other arithmetic, orthonormal(): return jax.scipy.linalg.solve_triangular(lower, matrix.T, lower=True).T  31.4 us
    all_to_all x1, waiting for transfers between devices, local(): lax.all_to_all(projected, 'gx', split_axis=0, concat_axis=1, tiled=True)  19.2 us
    dot_general x9, matrix products, product(): jnp.dot(left, right, precision=lax.Precision.HIGHEST, preferred_element_t...  18 us
  transfers between devices with their start and end apart: 2, of which 2 were waited for; matrix products, arithmetic and copies ran while one was open for 0% of the time, Pallas kernels for 0%

commit v1 on v0

v1 whole, which is shorter than its diff:
```python
import functools

import jax
import jax.numpy as jnp
from jax import lax
from jax.experimental import pallas as pl
from jax.experimental.pallas import tpu as pltpu
from jax.sharding import PartitionSpec as P

RANK = 128
ITERS = 2
NX = 512
GX, GY, GZ = 16, 8, 4
MESH = pl.DeviceIdType.MESH
VMEM = pltpu.VMEM
BLOCK = 128
NB = NX // BLOCK
PAIRS = [(i, j) for j in range(NB) for i in range(j, NB)]
PLANE = GY * GZ
PIECE = 24
HALF = PLANE * PIECE
PACKED = 2 * HALF
GROUPS = 5


def split(x):
    hi = x.astype(jnp.bfloat16)
    lo = (x - hi.astype(jnp.float32)).astype(jnp.bfloat16)
    return hi, lo


def contract(a, b, ca, cb):
    return lax.dot_general(a, b, (((ca,), (cb,)), ((), ())), preferred_element_type=jnp.float32)


def dot_split(a, b, ca=1, cb=0):
    (ah, al), (bh, bl) = a, b
    return contract(ah, bh, ca, cb) + (contract(ah, bl, ca, cb) + contract(al, bh, ca, cb))


def gather_gram_kernel(snap_ref, fib_ref, packed_ref, acc_ref, half_ref, parts_ref, levels_ref, own_ref,
                       send_sem, fib_sem, core_send, core_recv, part_send, part_recv,
                       level_send, level_recv, piece_send, piece_recv, back_send, back_recv):
    gx, gy, gz = lax.axis_index("gx"), lax.axis_index("gy"), lax.axis_index("gz")
    z, core = gx // 2, gx % 2
    rows = snap_ref.shape[1]
    ycount = fib_ref.shape[0]
    per = ycount // GROUPS
    partner = 2 * z + (1 - core)
    peers = []
    for dz in (4, 3, 5, 2, 6, 1, 7):
        for flip in (0, 1):
            peers.append(lax.rem(z + dz, 8) * 2 + (core if flip == 0 else 1 - core))
    peers.append(partner)
    plane = [(dy, dx) for dy in range(GY) for dx in range(GZ) if (dy, dx) != (0, 0)]

    def across(dy, dx):
        return lax.rem(gy + dy, GY), lax.rem(gz + dx, GZ)

    barrier = pltpu.get_barrier_semaphore()
    for peer in peers:
        pl.semaphore_signal(barrier, inc=1, device_id={"gx": peer}, device_id_type=MESH)
    for dy, dx in plane:
        ty, tx = across(dy, dx)
        pl.semaphore_signal(barrier, inc=1, device_id={"gy": ty, "gz": tx}, device_id_type=MESH)
    pl.semaphore_wait(barrier, len(peers) + len(plane))

    place = pl.ds(pl.multiple_of(gx * rows, rows), rows)
    for g in range(GROUPS):
        here = pl.ds(g * per, per)
        pltpu.make_async_copy(
            snap_ref.at[pl.ds(gx * ycount + g * per, per)], fib_ref.at[here, place], fib_sem.at[g]
        ).start()
        for peer in peers:
            pltpu.make_async_remote_copy(
                src_ref=snap_ref.at[pl.ds(peer * ycount + g * per, per)],
                dst_ref=fib_ref.at[here, place],
                send_sem=send_sem,
                recv_sem=fib_sem.at[g],
                device_id={"gx": peer},
                device_id_type=MESH,
            ).start()

    acc_ref[...] = jnp.zeros_like(acc_ref)
    for g in range(GROUPS):
        here = fib_ref.at[pl.ds(g * per, per)]
        pltpu.make_async_copy(here, here, fib_sem.at[g]).wait()
        for y in range(per):
            blocks = [split(fib_ref[g * per + y, pl.ds(b * BLOCK, BLOCK), :]) for b in range(NB)]
            for n, (i, j) in enumerate(PAIRS):
                at = pl.ds(n * BLOCK, BLOCK)
                acc_ref[at, :] += dot_split(blocks[i], blocks[j], 1, 1)
    sent = snap_ref.at[pl.ds(0, 15 * ycount)]
    pltpu.make_async_copy(sent, sent, send_sem).wait()

    mine = pl.multiple_of(core * HALF, HALF)
    other = pl.multiple_of((1 - core) * HALF, HALF)
    swap = pltpu.make_async_remote_copy(
        src_ref=acc_ref.at[pl.ds(other, HALF)], dst_ref=half_ref,
        send_sem=core_send, recv_sem=core_recv, device_id={"gx": partner}, device_id_type=MESH)
    swap.start()
    swap.wait()
    half_ref[...] += acc_ref[pl.ds(mine, HALF), :]

    slot = gy * GZ + gz
    for dy, dx in plane:
        ty, tx = across(dy, dx)
        theirs = ty * GZ + tx
        pltpu.make_async_remote_copy(
            src_ref=half_ref.at[pl.ds(pl.multiple_of(theirs * PIECE, 8), PIECE)],
            dst_ref=parts_ref.at[dy * GZ + dx - 1],
            send_sem=part_send, recv_sem=part_recv,
            device_id={"gy": ty, "gz": tx}, device_id_type=MESH).start()
    pieces = half_ref.at[pl.ds(0, len(plane) * PIECE)]
    pltpu.make_async_copy(pieces, pieces, part_send).wait()
    pltpu.make_async_copy(parts_ref, parts_ref, part_recv).wait()
    total = half_ref[pl.ds(pl.multiple_of(slot * PIECE, 8), PIECE), :]
    for n in range(len(plane)):
        total = total + parts_ref[n]
    own_ref[...] = total

    for dz in range(1, 8):
        pltpu.make_async_remote_copy(
            src_ref=own_ref, dst_ref=levels_ref.at[dz - 1],
            send_sem=level_send, recv_sem=level_recv,
            device_id={"gx": lax.rem(z + dz, 8) * 2 + core}, device_id_type=MESH).start()
    pieces = half_ref.at[pl.ds(0, 7 * PIECE)]
    pltpu.make_async_copy(pieces, pieces, level_send).wait()
    pltpu.make_async_copy(levels_ref, levels_ref, level_recv).wait()
    total = own_ref[...]
    start = own_ref[...]
    for level in range(8):
        pick = start
        for dz in range(1, 8):
            pick = jnp.where(lax.rem(level + dz, 8) == z, levels_ref[dz - 1], pick)
        total = pick if level == 0 else total + pick
    at = pl.ds(pl.multiple_of(mine + slot * PIECE, 8), PIECE)
    own_ref[...] = total
    packed_ref[at, :] = total

    for dy, dx in plane:
        ty, tx = across(dy, dx)
        pltpu.make_async_remote_copy(
            src_ref=own_ref, dst_ref=packed_ref.at[at],
            send_sem=piece_send, recv_sem=piece_recv,
            device_id={"gy": ty, "gz": tx}, device_id_type=MESH).start()
    pltpu.make_async_copy(parts_ref, parts_ref, piece_send).wait()
    pltpu.make_async_copy(parts_ref, parts_ref, piece_recv).wait()
    swap = pltpu.make_async_remote_copy(
        src_ref=packed_ref.at[pl.ds(mine, HALF)], dst_ref=packed_ref.at[pl.ds(mine, HALF)],
        send_sem=back_send, recv_sem=back_recv, device_id={"gx": partner}, device_id_type=MESH)
    swap.start()
    swap.wait()


def gather_gram(snap):
    ycount = snap.shape[0] // GX
    dma = pltpu.SemaphoreType.DMA
    return pl.pallas_call(
        gather_gram_kernel,
        out_shape=(jax.ShapeDtypeStruct((ycount, NX, BLOCK), jnp.float32),
                   jax.ShapeDtypeStruct((PACKED, BLOCK), jnp.float32)),
        in_specs=[pl.BlockSpec(memory_space=pl.ANY)],
        out_specs=(pl.BlockSpec(memory_space=VMEM), pl.BlockSpec(memory_space=VMEM)),
        scratch_shapes=[
            VMEM((PACKED, BLOCK), jnp.float32),
            VMEM((HALF, BLOCK), jnp.float32),
            VMEM((PLANE - 1, PIECE, BLOCK), jnp.float32),
            VMEM((7, PIECE, BLOCK), jnp.float32),
            VMEM((PIECE, BLOCK), jnp.float32),
            dma, dma((GROUPS,)), dma, dma, dma, dma, dma, dma, dma, dma, dma, dma,
        ],
        compiler_params=pltpu.CompilerParams(collective_id=0, has_side_effects=True),
    )(snap)


def inverse_factor(a):
    n = a.shape[0]
    tiles = [a[8 * t:8 * t + 8, :] for t in range(n // 8)]
    lane = lax.broadcasted_iota(jnp.int32, (8, n), 1)
    sub = lax.broadcasted_iota(jnp.int32, (8, n), 0)
    out = []
    for p in range(n // 8):
        base = 8 * p
        own = tiles[p]
        cols = [jnp.broadcast_to(own[:, base + j:base + j + 1], (8, n)) for j in range(8)]
        s = [[jnp.broadcast_to(cols[j][i:i + 1, :], (8, n)) for j in range(i + 1)] for i in range(8)]
        panel = (lane >= base) & (lane < base + 8)
        rows = [jnp.broadcast_to(own[j:j + 1, :], (8, n)) for j in range(8)]
        rows = [jnp.where(lane == base + j, 1.0, jnp.where(panel, 0.0, rows[j])) for j in range(8)]
        rinv, low = [], [[None] * 8 for _ in range(8)]
        for j in range(8):
            r = 1.0 / s[j][j]
            rinv.append(r)
            for i in range(j + 1, 8):
                low[i][j] = s[i][j] * r
            for i in range(j + 1, 8):
                for k in range(j + 1, i + 1):
                    s[i][k] = s[i][k] - low[i][j] * s[k][j]
        for j in range(8):
            for i in range(j):
                rows[j] = rows[j] - low[j][i] * rows[i]
        scaled = rows[0] * jnp.sqrt(rinv[0])
        for j in range(1, 8):
            scaled = jnp.where(sub == j, rows[j] * jnp.sqrt(rinv[j]), scaled)
        out.append(jnp.where(lane <= sub + base, scaled, 0.0))
        for t in range(p + 1, n // 8):
            tile = tiles[t]
            c = [jnp.broadcast_to(tile[:, base + j:base + j + 1], (8, n)) for j in range(8)]
            acc = jnp.where(panel, 0.0, tile)
            for j in range(8):
                for i in range(j):
                    c[j] = c[j] - c[i] * low[j][i]
            for j in range(8):
                acc = acc - (c[j] * rinv[j]) * rows[j]
            tiles[t] = acc
    return jnp.concatenate(out, axis=0)


def orth(m):
    m = split(m)
    return dot_split(m, split(inverse_factor(dot_split(m, m, 0, 0))), 1, 1)


def basis_kernel(packed_ref, basis_ref):
    blocks = {}
    for n, (i, j) in enumerate(PAIRS):
        blocks[i, j] = packed_ref[pl.ds(n * BLOCK, BLOCK), :]
    for i, j in PAIRS:
        if i != j:
            blocks[j, i] = blocks[i, j].T
    columns = [jnp.concatenate([blocks[i, j] for i in range(NB)], axis=0) for j in range(NB)]
    basis = orth(columns[0])
    gram = split(jnp.concatenate(columns, axis=1))
    for step in range(ITERS):
        basis = orth(dot_split(gram, split(basis)))
    basis_ref[...] = basis


def make_basis(packed):
    return pl.pallas_call(
        basis_kernel,
        out_shape=jax.ShapeDtypeStruct((NX, RANK), jnp.float32),
        in_specs=[pl.BlockSpec(memory_space=VMEM)],
        out_specs=pl.BlockSpec(memory_space=VMEM),
    )(packed)


def project_kernel(fib_ref, basis_ref, core_ref, mine_ref, sent_ref, send_sem, recv_sem):
    gx = lax.axis_index("gx")
    z, core = gx // 2, gx % 2
    ycount = fib_ref.shape[0]
    per = ycount // GROUPS
    ranks = core_ref.shape[1]
    rows = mine_ref.shape[0]
    peers = []
    for dz in (4, 3, 5, 2, 6, 1, 7):
        for flip in (0, 1):
            peers.append(lax.rem(z + dz, 8) * 2 + (core if flip == 0 else 1 - core))
    peers.append(2 * z + (1 - core))
    barrier = pltpu.get_barrier_semaphore()
    for peer in peers:
        pl.semaphore_signal(barrier, inc=1, device_id={"gx": peer}, device_id_type=MESH)
    mine_ref[...] = basis_ref[pl.ds(pl.multiple_of(gx * rows, rows), rows), :]
    basis = split(basis_ref[...])
    for g in range(GROUPS):
        for y in range(per):
            sent_ref[g * per + y] = dot_split(basis, split(fib_ref[g * per + y]), 0, 0)
        if g == 0:
            pl.semaphore_wait(barrier, len(peers))
        here = pl.ds(g * per, per)
        there = pl.ds(gx * ycount + g * per, per)
        for peer in peers:
            pltpu.make_async_remote_copy(
                src_ref=sent_ref.at[here, pl.ds(pl.multiple_of(peer * ranks, ranks), ranks)],
                dst_ref=core_ref.at[there],
                send_sem=send_sem, recv_sem=recv_sem,
                device_id={"gx": peer}, device_id_type=MESH).start()
        pltpu.make_async_copy(
            sent_ref.at[here, pl.ds(pl.multiple_of(gx * ranks, ranks), ranks)],
            core_ref.at[there], recv_sem).start()
    pltpu.make_async_copy(core_ref, core_ref, recv_sem).wait()
    done = core_ref.at[pl.ds(0, 15 * ycount)]
    pltpu.make_async_copy(done, done, send_sem).wait()


def project(fib, basis):
    ycount = fib.shape[0]
    return pl.pallas_call(
        project_kernel,
        out_shape=(jax.ShapeDtypeStruct((GX * ycount, RANK // GX, BLOCK), jnp.float32),
                   jax.ShapeDtypeStruct((NX // GX, RANK), jnp.float32)),
        in_specs=[pl.BlockSpec(memory_space=VMEM)] * 2,
        out_specs=(pl.BlockSpec(memory_space=VMEM),) * 2,
        scratch_shapes=[VMEM((ycount, RANK, BLOCK), jnp.float32),
                        pltpu.SemaphoreType.DMA, pltpu.SemaphoreType.DMA],
        compiler_params=pltpu.CompilerParams(collective_id=1, has_side_effects=True),
    )(fib, basis)


def local(snapshot):
    fib, packed = gather_gram(jnp.transpose(snapshot, (1, 0, 2)))
    basis = make_basis(packed)
    returned, mine = project(fib, basis)
    return (mine, jnp.transpose(returned, (1, 0, 2)))


def solution(mesh):
    in_specs = (P("gx", "gy", "gz"),)
    out_specs = (P("gx", None), P("gx", "gy", "gz"))
    return jax.shard_map(local, mesh=mesh, in_specs=in_specs, out_specs=out_specs, check_vma=False)
```

time: 584 us -> 162 us (0.28)
  waiting for transfers between devices: 291 us -> 0 us
  Pallas kernels: 0 us -> 153 us
  other arithmetic: 152 us -> 0 us
  blocking collectives: 73.8 us -> 0 us
  matrix products: 28.1 us -> 0 us
  between operations: 17.1 us -> 0.65 us
  starting transfers between devices: 6.06 us -> 0 us
    psum x1 -> x0, waiting for transfers between devices: 272 us -> none  [local(): factor = jnp.linalg.cholesky(lax.psum(gram, ('gx', 'gy', 'gz')))]
    pallas_call x0 -> x3, Pallas kernels: none -> 153 us  [the longest x1 111 us: gather_gram(): pl.pallas_call(gather_gram_kernel, out_shape=(jax.ShapeDtypeStruct((ycoun...]
    another operation x29 -> x0, other arithmetic: 149 us -> none  [the longest x14 80.6 us: local(): factor = jnp.linalg.cholesky(lax.psum(gram, ('gx', 'gy', 'gz')))]
    all_to_all x1 -> x0, blocking collectives: 73.8 us -> none  [local(): fibres = lax.all_to_all(flat, 'gx', split_axis=1, concat_axis=0, tiled=True)]
    all_to_all x1 -> x0, waiting for transfers between devices: 19.2 us -> none  [local(): lax.all_to_all(projected, 'gx', split_axis=0, concat_axis=1, tiled=True)]
    dot_general x9 -> x0, matrix products: 18 us -> none  [product(): jnp.dot(left, right, precision=lax.Precision.HIGHEST, preferred_element_t...]
    another operation x9 -> x0, matrix products: 10.1 us -> none  [the longest x6 7.83 us: local(): factor = jnp.linalg.cholesky(lax.psum(gram, ('gx', 'gy', 'gz')))]
    all_to_all x1 -> x0, starting transfers between devices: 6.02 us -> none  [local(): lax.all_to_all(projected, 'gx', split_axis=0, concat_axis=1, tiled=True)]
  transfers between devices with their start and end apart: 2 -> 0, of which waited for: 2 -> 0; matrix products, arithmetic and copies ran while one was open for 0% -> 0% of each run, Pallas kernels for 0% -> 0%
where the time goes in v1:
time: 162 us; the launch traced here: 161 us
  Pallas kernels  153 us (94%)
  local copies, waits for them, and re-layouts  8.15 us (5%)
    pallas_call x1, Pallas kernels, gather_gram(): pl.pallas_call(gather_gram_kernel, out_shape=(jax.ShapeDtypeStruct((ycoun...  111 us
    pallas_call x1, Pallas kernels, project(): pl.pallas_call(project_kernel, out_shape=(jax.ShapeDtypeStruct((GX * ycou...  21.8 us
    pallas_call x1, Pallas kernels, make_basis(): pl.pallas_call(basis_kernel, out_shape=jax.ShapeDtypeStruct((NX, RANK), j...  19.3 us
    unnamed x3, local copies, waits for them, and re-layouts  8.15 us

profile of v1, /device:TPU:1, one launch (start us, length us, event | category | flops | bytes accessed | tf_op | source)
XLA Modules:
  0.0 161.4 jit_solution(2842333380957648623)
XLA Ops:
  0.6 4.8 %copy.6 = f32[32,160,128]{2,0,1:T(8,128)} copy(f32[32,160,128]{2,1,0:T(8,128)} %param.1) | data formatting | bytes 5242880 | tf_op args[0]
  5.4 111.4 %shard_map.30 = (f32[10,512,128]{2,1,0:T(8,128)}, f32[1536,128]{1,0:T(8,128)}) custom-call(f32[160,32,128]{2,1,0:T(8,128)} %bitcast.4), custom_call_target="tpu_custom_call" | custom-call | tf_op jit(solution)/shard_map/pallas_call | solution.py:159
  116.8 19.3 %shard_map.31.basis_ref = f32[512,128]{1,0:T(8,128)} custom-call(f32[1536,128]{1,0:T(8,128)} %get-tuple-element.7.packed_ref), custom_call_target="tpu_custom_call" | custom-call | tf_op jit(solution)/shard_map/pallas_call | solution.py:241
  136.1 21.8 %shard_map.32 = (f32[160,8,128]{2,1,0:T(8,128)}, f32[32,128]{1,0:T(8,128)}) custom-call(f32[10,512,128]{2,1,0:T(8,128)} %get-tuple-element.6.fib_ref, f32[512,128]{1,0:T(8,128)} %shard_map.31.basis_ref), custom_call_target="tpu_custom_call" | custom-call | tf_op jit(solution)/shard_map/pallas_call | solution.py:289
  158.0 2.1 %copy.4 = f32[8,160,128]{2,1,0:T(8,128)} copy(f32[8,160,128]{2,0,1:T(8,128)} %bitcast.5) | data formatting | bytes 1310720
  160.0 1.3 copy.8

commit v2 on v0

v2 whole, which is shorter than its diff:
```python
import jax
import jax.numpy as jnp
from jax import lax
from jax.experimental import pallas as pl
from jax.experimental.pallas import tpu as pltpu
from jax.sharding import PartitionSpec as P

RANK = 128
ITERS = 2
NX = 512
GX, GY, GZ = 16, 8, 4
MESH = pl.DeviceIdType.MESH
VMEM = pltpu.VMEM
BLOCK = 128
PLANE = GY * GZ
EARLY, LATE = 24, 8
FIRST = EARLY * GX
EARLY_PIECE, LATE_PIECE = 16, 8
SPLIT = 2
STEPS = 10


def split(x):
    hi = x.astype(jnp.bfloat16)
    lo = (x - hi.astype(jnp.float32)).astype(jnp.bfloat16)
    return hi, lo


def contract(a, b, ca, cb):
    return lax.dot_general(a, b, (((ca,), (cb,)), ((), ())), preferred_element_type=jnp.float32)


def dot_split(a, b, ca=1, cb=0):
    (ah, al), (bh, bl) = a, b
    return contract(ah, bh, ca, cb) + (contract(ah, bl, ca, cb) + contract(al, bh, ca, cb))


def column_peers():
    gx = lax.axis_index("gx")
    z, core = gx // 2, gx % 2
    peers = [2 * z + (1 - core)]
    for dz in (1, 7, 2, 6, 3, 5, 4):
        peers.append(lax.rem(z + dz, 8) * 2 + core)
        peers.append(lax.rem(z + dz, 8) * 2 + (1 - core))
    return peers


class Sum:
    def __init__(self, piece, acc, half, parts, levels, own, out, sems):
        self.piece, self.acc, self.half, self.parts = piece, acc, half, parts
        self.levels, self.own, self.out, self.sems = levels, own, out, sems
        self.rows = PLANE * piece
        gx, gy, gz = lax.axis_index("gx"), lax.axis_index("gy"), lax.axis_index("gz")
        self.z, self.core = gx // 2, gx % 2
        self.partner = {"gx": 2 * self.z + (1 - self.core)}
        self.slot = gy * GZ + gz
        self.mine = pl.multiple_of(self.core * self.rows, self.rows)
        self.other = pl.multiple_of((1 - self.core) * self.rows, self.rows)
        self.plane = []
        for dy in range(GY):
            for dx in range(GZ):
                if (dy, dx) != (0, 0):
                    ty, tx = lax.rem(gy + dy, GY), lax.rem(gz + dx, GZ)
                    self.plane.append((dy * GZ + dx - 1, ty * GZ + tx, {"gy": ty, "gz": tx}))
        self.at = pl.ds(pl.multiple_of(self.mine + self.slot * piece, 8), piece)

    def copy(self, src, dst, step, device):
        return pltpu.make_async_remote_copy(
            src_ref=src, dst_ref=dst, send_sem=self.sems.at[2 * step], recv_sem=self.sems.at[2 * step + 1],
            device_id=device, device_id_type=MESH)

    def taken(self, step, count):
        gone = self.acc.at[pl.ds(0, count * self.piece)]
        pltpu.make_async_copy(gone, gone, self.sems.at[2 * step]).wait()
        pltpu.make_async_copy(gone, gone, self.sems.at[2 * step + 1]).wait()

    def swap(self):
        return self.copy(self.acc.at[pl.ds(self.other, self.rows)], self.half, 0, self.partner)

    def back(self):
        return self.copy(self.out.at[pl.ds(self.mine, self.rows)], self.out.at[pl.ds(self.mine, self.rows)],
                         4, self.partner)

    def start_cores(self):
        self.swap().start()

    def start_plane(self):
        self.swap().wait()
        self.half[...] += self.acc[pl.ds(self.mine, self.rows), :]
        for n, theirs, device in self.plane:
            src = self.half.at[pl.ds(pl.multiple_of(theirs * self.piece, 8), self.piece)]
            self.copy(src, self.parts.at[n], 1, device).start()

    def start_levels(self):
        self.taken(1, PLANE - 1)
        total = self.half[pl.ds(pl.multiple_of(self.slot * self.piece, 8), self.piece), :]
        for n in range(PLANE - 1):
            total = total + self.parts[n]
        self.own[0] = total
        for dz in range(1, 8):
            device = {"gx": lax.rem(self.z + dz, 8) * 2 + self.core}
            self.copy(self.own.at[0], self.levels.at[dz - 1], 2, device).start()

    def start_gather(self):
        self.taken(2, 7)
        total = self.own[0]
        for n in range(7):
            total = total + self.levels[n]
        self.own[1] = total
        self.out[self.at, :] = total
        for n, theirs, device in self.plane:
            self.copy(self.own.at[1], self.out.at[self.at], 3, device).start()

    def start_back(self):
        self.taken(3, PLANE - 1)
        self.back().start()

    def finish(self):
        self.back().wait()


def gather_gram_kernel(snap_ref, fib_out, early_out, late_out, fib_ref,
                       acc_e, half_e, parts_e, levels_e, own_e,
                       acc_l, half_l, parts_l, levels_l, own_l,
                       send_sem, fib_sem, keep_sem, sems_e, sems_l):
    gx = lax.axis_index("gx")
    ycount = fib_ref.shape[0]
    per = ycount // SPLIT
    peers = column_peers()
    early = Sum(EARLY_PIECE, acc_e, half_e, parts_e, levels_e, own_e, early_out, sems_e)
    late = Sum(LATE_PIECE, acc_l, half_l, parts_l, levels_l, own_l, late_out, sems_l)

    barrier = pltpu.get_barrier_semaphore()
    for peer in peers:
        pl.semaphore_signal(barrier, inc=1, device_id={"gx": peer}, device_id_type=MESH)
    for n, theirs, device in early.plane:
        pl.semaphore_signal(barrier, inc=1, device_id=device, device_id_type=MESH)
    pl.semaphore_wait(barrier, len(peers) + len(early.plane))

    for part, (first, count, base) in enumerate(((0, EARLY, 0), (EARLY, LATE, FIRST))):
        place = pl.ds(pl.multiple_of(base + gx * count, 8), count)
        for g in range(SPLIT):
            sem = fib_sem.at[part * SPLIT + g]

            def send(step, carry):
                y = g * per + step
                pltpu.make_async_copy(
                    snap_ref.at[pl.ds(first, count), gx * ycount + y], fib_ref.at[y, place], sem).start()
                for peer in peers:
                    pltpu.make_async_remote_copy(
                        src_ref=snap_ref.at[pl.ds(first, count), peer * ycount + y],
                        dst_ref=fib_ref.at[y, place],
                        send_sem=send_sem, recv_sem=sem,
                        device_id={"gx": peer}, device_id_type=MESH).start()
                return carry

            lax.fori_loop(0, per, send, 0)

    acc_e[...] = jnp.zeros_like(acc_e)
    acc_l[...] = jnp.zeros_like(acc_l)

    def arrived(part, g, base, rows):
        here = fib_ref.at[pl.ds(g * per, per), pl.ds(base, rows)]
        pltpu.make_async_copy(here, here, fib_sem.at[part * SPLIT + g]).wait()
        pltpu.make_async_copy(here, fib_out.at[pl.ds(g * per, per), pl.ds(base, rows)], keep_sem).start()

    def add_early(y, carry):
        hi, lo = split(fib_ref[y, pl.ds(0, FIRST), :])
        at = 0
        for j in range(FIRST // BLOCK):
            b = j * BLOCK
            rows = FIRST - b
            acc_e[pl.ds(at, rows), :] += dot_split(
                (hi[b:], lo[b:]), (hi[b:b + BLOCK], lo[b:b + BLOCK]), 1, 1)
            at += rows
        return carry

    def add_late(y, carry):
        hi, lo = split(fib_ref[y])
        acc_l[...] += dot_split((hi, lo), (hi[FIRST:], lo[FIRST:]), 1, 1)
        return carry

    for g in range(SPLIT):
        arrived(0, g, 0, FIRST)
        lax.fori_loop(g * per, g * per + per, add_early, 0)
    early.start_cores()
    early.start_plane()
    early.start_levels()
    for g in range(SPLIT):
        arrived(1, g, FIRST, NX - FIRST)
        lax.fori_loop(g * per, g * per + per, add_late, 0)
    late.start_cores()
    late.start_plane()
    early.start_gather()
    late.start_levels()
    early.start_back()
    late.start_gather()
    early.finish()
    late.start_back()
    sent = fib_ref.at[:, pl.ds(0, NX - NX // GX)]
    pltpu.make_async_copy(sent, sent, send_sem).wait()
    pltpu.make_async_copy(fib_ref, fib_out, keep_sem).wait()
    late.finish()


def gather_gram(snap):
    ycount = snap.shape[1] // GX
    dma = pltpu.SemaphoreType.DMA

    def scratch(piece):
        rows = PLANE * piece
        return [VMEM((2 * rows, BLOCK), jnp.float32), VMEM((rows, BLOCK), jnp.float32),
                VMEM((PLANE - 1, piece, BLOCK), jnp.float32), VMEM((7, piece, BLOCK), jnp.float32),
                VMEM((2, piece, BLOCK), jnp.float32)]

    return pl.pallas_call(
        gather_gram_kernel,
        out_shape=(jax.ShapeDtypeStruct((ycount, NX, BLOCK), jnp.float32),
                   jax.ShapeDtypeStruct((2 * PLANE * EARLY_PIECE, BLOCK), jnp.float32),
                   jax.ShapeDtypeStruct((2 * PLANE * LATE_PIECE, BLOCK), jnp.float32)),
        in_specs=[pl.BlockSpec(memory_space=pl.ANY)],
        out_specs=(pl.BlockSpec(memory_space=pl.ANY), pl.BlockSpec(memory_space=VMEM),
                   pl.BlockSpec(memory_space=VMEM)),
        scratch_shapes=[VMEM((ycount, NX, BLOCK), jnp.float32)] + scratch(EARLY_PIECE) + scratch(LATE_PIECE)
        + [dma, dma((2 * SPLIT,)), dma, dma((STEPS,)), dma((STEPS,))],
        compiler_params=pltpu.CompilerParams(collective_id=0, has_side_effects=True),
    )(snap)


def inverse_factor(a):
    n = a.shape[0]
    tiles = [a[8 * t:8 * t + 8, :] for t in range(n // 8)]
    lane = lax.broadcasted_iota(jnp.int32, (8, n), 1)
    sub = lax.broadcasted_iota(jnp.int32, (8, n), 0)
    out = []
    for p in range(n // 8):
        base = 8 * p
        own = tiles[p]
        cols = [jnp.broadcast_to(own[:, base + j:base + j + 1], (8, n)) for j in range(8)]
        s = [[jnp.broadcast_to(cols[j][i:i + 1, :], (8, n)) for j in range(i + 1)] for i in range(8)]
        panel = (lane >= base) & (lane < base + 8)
        rows = [jnp.broadcast_to(own[j:j + 1, :], (8, n)) for j in range(8)]
        rows = [jnp.where(lane == base + j, 1.0, jnp.where(panel, 0.0, rows[j])) for j in range(8)]
        rinv, low = [], [[None] * 8 for _ in range(8)]
        for j in range(8):
            r = 1.0 / s[j][j]
            rinv.append(r)
            for i in range(j + 1, 8):
                low[i][j] = s[i][j] * r
            for i in range(j + 1, 8):
                for k in range(j + 1, i + 1):
                    s[i][k] = s[i][k] - low[i][j] * s[k][j]
        for j in range(8):
            for i in range(j):
                rows[j] = rows[j] - low[j][i] * rows[i]
        scaled = rows[0] * jnp.sqrt(rinv[0])
        for j in range(1, 8):
            scaled = jnp.where(sub == j, rows[j] * jnp.sqrt(rinv[j]), scaled)
        out.append(jnp.where(lane <= sub + base, scaled, 0.0))
        for t in range(p + 1, n // 8):
            tile = tiles[t]
            c = [jnp.broadcast_to(tile[:, base + j:base + j + 1], (8, n)) for j in range(8)]
            acc = jnp.where(panel, 0.0, tile)
            for j in range(8):
                for i in range(j):
                    c[j] = c[j] - c[i] * low[j][i]
            for j in range(8):
                acc = acc - (c[j] * rinv[j]) * rows[j]
            tiles[t] = acc
    return jnp.concatenate(out, axis=0)


def basis_project_kernel(early_ref, late_ref, fib_hbm, core_ref, mine_ref, fib_ref, hi_ref, lo_ref,
                         m_ref, bt_ref, b_ref, sent_ref, fib_sem, send_sem, recv_sem):
    gx = lax.axis_index("gx")
    ycount = fib_ref.shape[0]
    ranks = core_ref.shape[1]
    peers = column_peers()
    barrier = pltpu.get_barrier_semaphore()
    for peer in peers:
        pl.semaphore_signal(barrier, inc=1, device_id={"gx": peer}, device_id_type=MESH)
    load = pltpu.make_async_copy(fib_hbm, fib_ref, fib_sem)
    load.start()

    nb = NX // BLOCK
    blocks, at = {}, 0
    for j in range(nb - 1):
        for i in range(j, nb - 1):
            blocks[i, j] = early_ref[pl.ds(at, BLOCK), :]
            at += BLOCK
    for i in range(nb):
        blocks[i, nb - 1] = late_ref[pl.ds(i * BLOCK, BLOCK), :]
    for i in range(nb):
        for j in range(nb):
            if (i, j) not in blocks:
                blocks[i, j] = blocks[j, i].T
    rows = [jnp.concatenate([blocks[i, j] for j in range(nb)], axis=1) for i in range(nb)]
    for i in range(nb):
        hi, lo = split(rows[i])
        hi_ref[pl.ds(i * BLOCK, BLOCK), :] = hi
        lo_ref[pl.ds(i * BLOCK, BLOCK), :] = lo
    per_block = RANK // (EARLY + LATE)
    for n in range(per_block):
        m_ref[pl.ds(n * (EARLY + LATE), EARLY), :] = rows[0][n * EARLY:(n + 1) * EARLY]
        m_ref[pl.ds(n * (EARLY + LATE) + EARLY, LATE), :] = rows[nb - 1][n * LATE:(n + 1) * LATE]

    def iterate(step, carry):
        m = split(m_ref[...])
        basis = dot_split(split(inverse_factor(dot_split(m, m, 1, 1))), m)
        bt_ref[...] = basis

        @pl.when(step < ITERS)
        def _():
            m_ref[...] = dot_split(split(basis), (hi_ref[...], lo_ref[...]))

        return carry

    lax.fori_loop(0, ITERS + 1, iterate, 0)
    basis = split(bt_ref[...])
    load.wait()
    pl.semaphore_wait(barrier, len(peers))

    def emit(y, carry):
        sent_ref[y] = dot_split(basis, split(fib_ref[y]))
        there = core_ref.at[gx * ycount + y]
        for peer in peers:
            pltpu.make_async_remote_copy(
                src_ref=sent_ref.at[y, pl.ds(pl.multiple_of(peer * ranks, ranks), ranks)],
                dst_ref=there, send_sem=send_sem, recv_sem=recv_sem,
                device_id={"gx": peer}, device_id_type=MESH).start()
        pltpu.make_async_copy(
            sent_ref.at[y, pl.ds(pl.multiple_of(gx * ranks, ranks), ranks)], there, recv_sem).start()
        return carry

    lax.fori_loop(0, ycount, emit, 0)
    b_ref[...] = bt_ref[...].T
    mine_ref[pl.ds(0, EARLY), :] = b_ref[pl.ds(pl.multiple_of(gx * EARLY, 8), EARLY), :]
    mine_ref[pl.ds(EARLY, LATE), :] = b_ref[pl.ds(pl.multiple_of(FIRST + gx * LATE, 8), LATE), :]
    done = sent_ref.at[:, pl.ds(0, RANK - RANK // GX)]
    pltpu.make_async_copy(done, done, send_sem).wait()
    pltpu.make_async_copy(core_ref, core_ref, recv_sem).wait()


def basis_project(fib, early, late):
    ycount = fib.shape[0]
    dma = pltpu.SemaphoreType.DMA
    return pl.pallas_call(
        basis_project_kernel,
        out_shape=(jax.ShapeDtypeStruct((GX * ycount, RANK // GX, BLOCK), jnp.float32),
                   jax.ShapeDtypeStruct((NX // GX, RANK), jnp.float32)),
        in_specs=[pl.BlockSpec(memory_space=VMEM)] * 2 + [pl.BlockSpec(memory_space=pl.ANY)],
        out_specs=(pl.BlockSpec(memory_space=VMEM),) * 2,
        scratch_shapes=[VMEM((ycount, NX, BLOCK), jnp.float32),
                        VMEM((NX, NX), jnp.bfloat16), VMEM((NX, NX), jnp.bfloat16),
                        VMEM((RANK, NX), jnp.float32), VMEM((RANK, NX), jnp.float32),
                        VMEM((NX, RANK), jnp.float32), VMEM((ycount, RANK, BLOCK), jnp.float32),
                        dma, dma, dma],
        compiler_params=pltpu.CompilerParams(collective_id=1, has_side_effects=True),
    )(early, late, fib)


def local(snapshot):
    fib, early, late = gather_gram(snapshot)
    returned, mine = basis_project(fib, early, late)
    return (mine, jnp.transpose(returned, (1, 0, 2)))


def solution(mesh):
    in_specs = (P("gx", "gy", "gz"),)
    out_specs = (P("gx", None), P("gx", "gy", "gz"))
    return jax.shard_map(local, mesh=mesh, in_specs=in_specs, out_specs=out_specs, check_vma=False)
```

time: 584 us -> 142 us (0.24)
  waiting for transfers between devices: 291 us -> 0 us
  other arithmetic: 152 us -> 0 us
  Pallas kernels: 0 us -> 138 us
  blocking collectives: 73.8 us -> 0 us
  matrix products: 28.1 us -> 0 us
  between operations: 17.1 us -> 0.65 us
  local copies, waits for them, and re-layouts: 12 us -> 3.37 us
  starting transfers between devices: 6.06 us -> 0 us
    psum x1 -> x0, waiting for transfers between devices: 272 us -> none  [local(): factor = jnp.linalg.cholesky(lax.psum(gram, ('gx', 'gy', 'gz')))]
    another operation x29 -> x0, other arithmetic: 149 us -> none  [the longest x14 80.6 us: local(): factor = jnp.linalg.cholesky(lax.psum(gram, ('gx', 'gy', 'gz')))]
    pallas_call x0 -> x2, Pallas kernels: none -> 138 us  [the longest x1 101 us: gather_gram(): pl.pallas_call(gather_gram_kernel, out_shape=(jax.ShapeDtypeStruct((ycoun...]
    all_to_all x1 -> x0, blocking collectives: 73.8 us -> none  [local(): fibres = lax.all_to_all(flat, 'gx', split_axis=1, concat_axis=0, tiled=True)]
    all_to_all x1 -> x0, waiting for transfers between devices: 19.2 us -> none  [local(): lax.all_to_all(projected, 'gx', split_axis=0, concat_axis=1, tiled=True)]
    dot_general x9 -> x0, matrix products: 18 us -> none  [product(): jnp.dot(left, right, precision=lax.Precision.HIGHEST, preferred_element_t...]
    another operation x9 -> x0, matrix products: 10.1 us -> none  [the longest x6 7.83 us: local(): factor = jnp.linalg.cholesky(lax.psum(gram, ('gx', 'gy', 'gz')))]
    all_to_all x1 -> x0, starting transfers between devices: 6.02 us -> none  [local(): lax.all_to_all(projected, 'gx', split_axis=0, concat_axis=1, tiled=True)]
  transfers between devices with their start and end apart: 2 -> 0, of which waited for: 2 -> 0; matrix products, arithmetic and copies ran while one was open for 0% -> 0% of each run, Pallas kernels for 0% -> 0%
where the time goes in v2:
time: 142 us
  Pallas kernels  138 us (97%)
  local copies, waits for them, and re-layouts  3.37 us (2%)
    pallas_call x1, Pallas kernels, gather_gram(): pl.pallas_call(gather_gram_kernel, out_shape=(jax.ShapeDtypeStruct((ycoun...  101 us
    pallas_call x1, Pallas kernels, basis_project(): pl.pallas_call(basis_project_kernel, out_shape=(jax.ShapeDtypeStruct((GX...  37 us
    unnamed x2, local copies, waits for them, and re-layouts  3.37 us

profile of v2, /device:TPU:1, one launch (start us, length us, event | category | flops | bytes accessed | tf_op | source)
XLA Modules:
  0.0 142.1 jit_solution(17866107192860502412)
XLA Ops:
  0.6 101.1 %shard_map.30 = (f32[10,512,128]{2,1,0:T(8,128)}, f32[1024,128]{1,0:T(8,128)}, f32[512,128]{1,0:T(8,128)}) custom-call(f32[32,160,128]{2,1,0:T(8,128)} %snap_ref.1), custom_call_target="tpu_custom_call" | custom-call | tf_op jit(solution)/shard_map/pallas_call | solution.py:216
  101.7 37.0 %shard_map.31 = (f32[160,8,128]{2,1,0:T(8,128)}, f32[32,128]{1,0:T(8,128)}) custom-call(f32[1024,128]{1,0:T(8,128)} %get-tuple-element.7.early_ref, f32[512,128]{1,0:T(8,128)} %get-tuple-element.8.late_ref, f32[10,512,128]{2,1,0:T(8,128)} %get-tuple-element.9.fib_hbm), custom_call_target="tpu_custom_call" | custom-call | tf_op jit(solution)/shard_map/pallas_call | solution.py:347
  138.7 2.1 %copy.3 = f32[8,160,128]{2,1,0:T(8,128)} copy(f32[8,160,128]{2,0,1:T(8,128)} %bitcast.1) | data formatting | bytes 1310720
  140.8 1.3 copy.5

commit v3 on v2

--- a/solution.py
+++ b/solution.py
@@ -16,7 +16,7 @@
 EARLY, LATE = 24, 8
 FIRST = EARLY * GX
 EARLY_PIECE, LATE_PIECE = 16, 8
-SPLIT = 2
+SPLIT = 5
 STEPS = 10
 
 
@@ -137,32 +137,51 @@
         pl.semaphore_signal(barrier, inc=1, device_id=device, device_id_type=MESH)
     pl.semaphore_wait(barrier, len(peers) + len(early.plane))
 
-    for part, (first, count, base) in enumerate(((0, EARLY, 0), (EARLY, LATE, FIRST))):
-        place = pl.ds(pl.multiple_of(base + gx * count, 8), count)
-        for g in range(SPLIT):
-            sem = fib_sem.at[part * SPLIT + g]
-
-            def send(step, carry):
+    place = pl.ds(pl.multiple_of(gx * EARLY, 8), EARLY)
+    late_place = pl.ds(pl.multiple_of(FIRST + gx * LATE, 8), LATE)
+
+    def keep(y, carry):
+        column = gx * ycount + y
+        pltpu.make_async_copy(
+            snap_ref.at[pl.ds(0, EARLY), column], fib_ref.at[y, place], fib_sem.at[0]).start()
+        pltpu.make_async_copy(
+            snap_ref.at[pl.ds(EARLY, LATE), column], fib_ref.at[y, late_place], fib_sem.at[1 + y // per]).start()
+        return carry
+
+    for peer in peers:
+
+        def send(y, carry):
+            pltpu.make_async_remote_copy(
+                src_ref=snap_ref.at[pl.ds(0, EARLY), peer * ycount + y],
+                dst_ref=fib_ref.at[y, place],
+                send_sem=send_sem, recv_sem=fib_sem.at[0],
+                device_id={"gx": peer}, device_id_type=MESH).start()
+            return carry
+
+        lax.fori_loop(0, ycount, send, 0)
+
+    def send_late(g, carry):
+        for peer in peers:
+            for step in range(per):
                 y = g * per + step
-                pltpu.make_async_copy(
-                    snap_ref.at[pl.ds(first, count), gx * ycount + y], fib_ref.at[y, place], sem).start()
-                for peer in peers:
-                    pltpu.make_async_remote_copy(
-                        src_ref=snap_ref.at[pl.ds(first, count), peer * ycount + y],
-                        dst_ref=fib_ref.at[y, place],
-                        send_sem=send_sem, recv_sem=sem,
-                        device_id={"gx": peer}, device_id_type=MESH).start()
-                return carry
-
-            lax.fori_loop(0, per, send, 0)
+                pltpu.make_async_remote_copy(
+                    src_ref=snap_ref.at[pl.ds(EARLY, LATE), peer * ycount + y],
+                    dst_ref=fib_ref.at[y, late_place],
+                    send_sem=send_sem, recv_sem=fib_sem.at[1 + g],
+                    device_id={"gx": peer}, device_id_type=MESH).start()
+        return carry
+
+    lax.fori_loop(0, SPLIT, send_late, 0)
+    lax.fori_loop(0, ycount, keep, 0)
 
     acc_e[...] = jnp.zeros_like(acc_e)
     acc_l[...] = jnp.zeros_like(acc_l)
 
-    def arrived(part, g, base, rows):
-        here = fib_ref.at[pl.ds(g * per, per), pl.ds(base, rows)]
-        pltpu.make_async_copy(here, here, fib_sem.at[part * SPLIT + g]).wait()
-        pltpu.make_async_copy(here, fib_out.at[pl.ds(g * per, per), pl.ds(base, rows)], keep_sem).start()
+    def arrived(sem, first, count, base, rows):
+        ys, xs = pl.ds(first, count), pl.ds(base, rows)
+        here = fib_ref.at[ys, xs]
+        pltpu.make_async_copy(here, here, fib_sem.at[sem]).wait()
+        pltpu.make_async_copy(here, fib_out.at[ys, xs], keep_sem).start()
 
     def add_early(y, carry):
         hi, lo = split(fib_ref[y, pl.ds(0, FIRST), :])
@@ -180,23 +199,25 @@
         acc_l[...] += dot_split((hi, lo), (hi[FIRST:], lo[FIRST:]), 1, 1)
         return carry
 
-    for g in range(SPLIT):
-        arrived(0, g, 0, FIRST)
-        lax.fori_loop(g * per, g * per + per, add_early, 0)
+    arrived(0, 0, ycount, 0, FIRST)
+    lax.fori_loop(0, ycount, add_early, 0)
     early.start_cores()
     early.start_plane()
     early.start_levels()
-    for g in range(SPLIT):
-        arrived(1, g, FIRST, NX - FIRST)
-        lax.fori_loop(g * per, g * per + per, add_late, 0)
+
+    def take_late(g, carry):
+        arrived(1 + g, g * per, per, FIRST, NX - FIRST)
+        return lax.fori_loop(g * per, g * per + per, add_late, carry)
+
+    lax.fori_loop(0, SPLIT, take_late, 0)
     late.start_cores()
     late.start_plane()
+    late.start_levels()
     early.start_gather()
-    late.start_levels()
+    late.start_gather()
     early.start_back()
-    late.start_gather()
+    late.start_back()
     early.finish()
-    late.start_back()
     sent = fib_ref.at[:, pl.ds(0, NX - NX // GX)]
     pltpu.make_async_copy(sent, sent, send_sem).wait()
     pltpu.make_async_copy(fib_ref, fib_out, keep_sem).wait()
@@ -222,51 +243,57 @@
         out_specs=(pl.BlockSpec(memory_space=pl.ANY), pl.BlockSpec(memory_space=VMEM),
                    pl.BlockSpec(memory_space=VMEM)),
         scratch_shapes=[VMEM((ycount, NX, BLOCK), jnp.float32)] + scratch(EARLY_PIECE) + scratch(LATE_PIECE)
-        + [dma, dma((2 * SPLIT,)), dma, dma((STEPS,)), dma((STEPS,))],
+        + [dma, dma((1 + SPLIT,)), dma, dma((STEPS,)), dma((STEPS,))],
         compiler_params=pltpu.CompilerParams(collective_id=0, has_side_effects=True),
     )(snap)
 
 
 def inverse_factor(a):
     n = a.shape[0]
-    tiles = [a[8 * t:8 * t + 8, :] for t in range(n // 8)]
+    count = n // 8
+    tiles = [a[8 * t:8 * t + 8, :] for t in range(count)]
     lane = lax.broadcasted_iota(jnp.int32, (8, n), 1)
     sub = lax.broadcasted_iota(jnp.int32, (8, n), 0)
+    spread = lane - sub
     out = []
-    for p in range(n // 8):
+    for p in range(count):
         base = 8 * p
         own = tiles[p]
-        cols = [jnp.broadcast_to(own[:, base + j:base + j + 1], (8, n)) for j in range(8)]
+        cols = [jnp.take_along_axis(own, jnp.full((8, n), base + j, jnp.int32), axis=1) for j in range(8)]
         s = [[jnp.broadcast_to(cols[j][i:i + 1, :], (8, n)) for j in range(i + 1)] for i in range(8)]
         panel = (lane >= base) & (lane < base + 8)
-        rows = [jnp.broadcast_to(own[j:j + 1, :], (8, n)) for j in range(8)]
-        rows = [jnp.where(lane == base + j, 1.0, jnp.where(panel, 0.0, rows[j])) for j in range(8)]
+        ready = jnp.where(panel, jnp.where(spread == base, 1.0, 0.0), own)
+        rows = [jnp.broadcast_to(ready[j:j + 1, :], (8, n)) for j in range(8)]
         rinv, low = [], [[None] * 8 for _ in range(8)]
         for j in range(8):
             r = 1.0 / s[j][j]
             rinv.append(r)
             for i in range(j + 1, 8):
                 low[i][j] = s[i][j] * r
-            for i in range(j + 1, 8):
                 for k in range(j + 1, i + 1):
                     s[i][k] = s[i][k] - low[i][j] * s[k][j]
+                rows[i] = rows[i] - low[i][j] * rows[j]
+        merged, pivots = rows[0], s[0][0]
+        for j in range(1, 8):
+            merged = jnp.where(sub == j, rows[j], merged)
+            pivots = jnp.where(sub == j, s[j][j], pivots)
+        out.append(jnp.where(spread <= base, merged * lax.rsqrt(pivots), 0.0))
+        if p + 1 == count:
+            break
+        solved = [rows[j] * rinv[j] for j in range(8)]
+        for j in range(7, 0, -1):
+            for i in range(j):
+                solved[i] = solved[i] - low[j][i] * solved[j]
+        rest = range(p + 1, count)
+        acc = {t: jnp.where(panel, 0.0, tiles[t]) for t in rest}
+        first = p + 1
         for j in range(8):
-            for i in range(j):
-                rows[j] = rows[j] - low[j][i] * rows[i]
-        scaled = rows[0] * jnp.sqrt(rinv[0])
-        for j in range(1, 8):
-            scaled = jnp.where(sub == j, rows[j] * jnp.sqrt(rinv[j]), scaled)
-        out.append(jnp.where(lane <= sub + base, scaled, 0.0))
-        for t in range(p + 1, n // 8):
-            tile = tiles[t]
-            c = [jnp.broadcast_to(tile[:, base + j:base + j + 1], (8, n)) for j in range(8)]
-            acc = jnp.where(panel, 0.0, tile)
+            acc[first] = acc[first] - jnp.broadcast_to(tiles[first][:, base + j:base + j + 1], (8, n)) * solved[j]
+        for t in range(p + 2, count):
             for j in range(8):
-                for i in range(j):
-                    c[j] = c[j] - c[i] * low[j][i]
-            for j in range(8):
-                acc = acc - (c[j] * rinv[j]) * rows[j]
-            tiles[t] = acc
+                acc[t] = acc[t] - jnp.broadcast_to(tiles[t][:, base + j:base + j + 1], (8, n)) * solved[j]
+        for t in rest:
+            tiles[t] = acc[t]
     return jnp.concatenate(out, axis=0)
 
 

time: 142 us -> 147 us (1.035)
  Pallas kernels: 138 us -> 143 us
    pallas_call x1, Pallas kernels: 101 us -> 106 us  [gather_gram(): pl.pallas_call(gather_gram_kernel, out_shape=(jax.ShapeDtypeStruct((ycoun...]
where the time goes in v3:
time: 147 us
  Pallas kernels  143 us (97%)
  local copies, waits for them, and re-layouts  3.37 us (2%)
    pallas_call x1, Pallas kernels, gather_gram(): pl.pallas_call(gather_gram_kernel, out_shape=(jax.ShapeDtypeStruct((ycoun...  106 us
    pallas_call x1, Pallas kernels, basis_project(): pl.pallas_call(basis_project_kernel, out_shape=(jax.ShapeDtypeStruct((GX...  36.2 us
    unnamed x2, local copies, waits for them, and re-layouts  3.37 us

profile of v3, /device:TPU:1, one launch (start us, length us, event | category | flops | bytes accessed | tf_op | source)
XLA Modules:
  0.0 146.7 jit_solution(10743465352383542604)
XLA Ops:
  0.6 106.5 %shard_map.30 = (f32[10,512,128]{2,1,0:T(8,128)}, f32[1024,128]{1,0:T(8,128)}, f32[512,128]{1,0:T(8,128)}) custom-call(f32[32,160,128]{2,1,0:T(8,128)} %snap_ref.1), custom_call_target="tpu_custom_call" | custom-call | tf_op jit(solution)/shard_map/pallas_call | solution.py:237
  107.1 36.2 %shard_map.31 = (f32[160,8,128]{2,1,0:T(8,128)}, f32[32,128]{1,0:T(8,128)}) custom-call(f32[1024,128]{1,0:T(8,128)} %get-tuple-element.7.early_ref, f32[512,128]{1,0:T(8,128)} %get-tuple-element.8.late_ref, f32[10,512,128]{2,1,0:T(8,128)} %get-tuple-element.9.fib_hbm), custom_call_target="tpu_custom_call" | custom-call | tf_op jit(solution)/shard_map/pallas_call | solution.py:374
  143.3 2.1 %copy.3 = f32[8,160,128]{2,1,0:T(8,128)} copy(f32[8,160,128]{2,0,1:T(8,128)} %bitcast.1) | data formatting | bytes 1310720
  145.4 1.3 copy.5

commit v4 on v3

--- a/solution.py
+++ b/solution.py
@@ -39,9 +39,12 @@
     gx = lax.axis_index("gx")
     z, core = gx // 2, gx % 2
     peers = [2 * z + (1 - core)]
-    for dz in (1, 7, 2, 6, 3, 5, 4):
-        peers.append(lax.rem(z + dz, 8) * 2 + core)
-        peers.append(lax.rem(z + dz, 8) * 2 + (1 - core))
+    for distance in (1, 2, 3):
+        for side in (core, 1 - core):
+            for dz in (distance, 8 - distance):
+                peers.append(lax.rem(z + dz, 8) * 2 + side)
+    for side in (core, 1 - core):
+        peers.append(lax.rem(z + 4, 8) * 2 + side)
     return peers
 
 
@@ -137,50 +140,30 @@
         pl.semaphore_signal(barrier, inc=1, device_id=device, device_id_type=MESH)
     pl.semaphore_wait(barrier, len(peers) + len(early.plane))
 
-    place = pl.ds(pl.multiple_of(gx * EARLY, 8), EARLY)
-    late_place = pl.ds(pl.multiple_of(FIRST + gx * LATE, 8), LATE)
-
-    def keep(y, carry):
-        column = gx * ycount + y
-        pltpu.make_async_copy(
-            snap_ref.at[pl.ds(0, EARLY), column], fib_ref.at[y, place], fib_sem.at[0]).start()
-        pltpu.make_async_copy(
-            snap_ref.at[pl.ds(EARLY, LATE), column], fib_ref.at[y, late_place], fib_sem.at[1 + y // per]).start()
-        return carry
-
-    for peer in peers:
+    for part, (first, count, base) in enumerate(((0, EARLY, 0), (EARLY, LATE, FIRST))):
+        place = pl.ds(pl.multiple_of(base + gx * count, 8), count)
 
         def send(y, carry):
-            pltpu.make_async_remote_copy(
-                src_ref=snap_ref.at[pl.ds(0, EARLY), peer * ycount + y],
-                dst_ref=fib_ref.at[y, place],
-                send_sem=send_sem, recv_sem=fib_sem.at[0],
-                device_id={"gx": peer}, device_id_type=MESH).start()
+            sem = fib_sem.at[part * SPLIT + y // per]
+            pltpu.make_async_copy(
+                snap_ref.at[pl.ds(first, count), gx * ycount + y], fib_ref.at[y, place], sem).start()
+            for peer in peers:
+                pltpu.make_async_remote_copy(
+                    src_ref=snap_ref.at[pl.ds(first, count), peer * ycount + y],
+                    dst_ref=fib_ref.at[y, place],
+                    send_sem=send_sem, recv_sem=sem,
+                    device_id={"gx": peer}, device_id_type=MESH).start()
             return carry
 
         lax.fori_loop(0, ycount, send, 0)
-
-    def send_late(g, carry):
-        for peer in peers:
-            for step in range(per):
-                y = g * per + step
-                pltpu.make_async_remote_copy(
-                    src_ref=snap_ref.at[pl.ds(EARLY, LATE), peer * ycount + y],
-                    dst_ref=fib_ref.at[y, late_place],
-                    send_sem=send_sem, recv_sem=fib_sem.at[1 + g],
-                    device_id={"gx": peer}, device_id_type=MESH).start()
-        return carry
-
-    lax.fori_loop(0, SPLIT, send_late, 0)
-    lax.fori_loop(0, ycount, keep, 0)
 
     acc_e[...] = jnp.zeros_like(acc_e)
     acc_l[...] = jnp.zeros_like(acc_l)
 
-    def arrived(sem, first, count, base, rows):
-        ys, xs = pl.ds(first, count), pl.ds(base, rows)
+    def arrived(part, g, base, rows):
+        ys, xs = pl.ds(g * per, per), pl.ds(base, rows)
         here = fib_ref.at[ys, xs]
-        pltpu.make_async_copy(here, here, fib_sem.at[sem]).wait()
+        pltpu.make_async_copy(here, here, fib_sem.at[part * SPLIT + g]).wait()
         pltpu.make_async_copy(here, fib_out.at[ys, xs], keep_sem).start()
 
     def add_early(y, carry):
@@ -199,14 +182,17 @@
         acc_l[...] += dot_split((hi, lo), (hi[FIRST:], lo[FIRST:]), 1, 1)
         return carry
 
-    arrived(0, 0, ycount, 0, FIRST)
-    lax.fori_loop(0, ycount, add_early, 0)
+    def take_early(g, carry):
+        arrived(0, g, 0, FIRST)
+        return lax.fori_loop(g * per, g * per + per, add_early, carry)
+
+    lax.fori_loop(0, SPLIT, take_early, 0)
     early.start_cores()
     early.start_plane()
     early.start_levels()
 
     def take_late(g, carry):
-        arrived(1 + g, g * per, per, FIRST, NX - FIRST)
+        arrived(1, g, FIRST, NX - FIRST)
         return lax.fori_loop(g * per, g * per + per, add_late, carry)
 
     lax.fori_loop(0, SPLIT, take_late, 0)
@@ -243,7 +229,7 @@
         out_specs=(pl.BlockSpec(memory_space=pl.ANY), pl.BlockSpec(memory_space=VMEM),
                    pl.BlockSpec(memory_space=VMEM)),
         scratch_shapes=[VMEM((ycount, NX, BLOCK), jnp.float32)] + scratch(EARLY_PIECE) + scratch(LATE_PIECE)
-        + [dma, dma((1 + SPLIT,)), dma, dma((STEPS,)), dma((STEPS,))],
+        + [dma, dma((2 * SPLIT,)), dma, dma((STEPS,)), dma((STEPS,))],
         compiler_params=pltpu.CompilerParams(collective_id=0, has_side_effects=True),
     )(snap)
 
@@ -301,7 +287,7 @@
                          m_ref, bt_ref, b_ref, sent_ref, fib_sem, send_sem, recv_sem):
     gx = lax.axis_index("gx")
     ycount = fib_ref.shape[0]
-    ranks = core_ref.shape[1]
+    ranks = core_ref.shape[0]
     peers = column_peers()
     barrier = pltpu.get_barrier_semaphore()
     for peer in peers:
@@ -349,7 +335,7 @@
 
     def emit(y, carry):
         sent_ref[y] = dot_split(basis, split(fib_ref[y]))
-        there = core_ref.at[gx * ycount + y]
+        there = core_ref.at[:, gx * ycount + y]
         for peer in peers:
             pltpu.make_async_remote_copy(
                 src_ref=sent_ref.at[y, pl.ds(pl.multiple_of(peer * ranks, ranks), ranks)],
@@ -373,7 +359,7 @@
     dma = pltpu.SemaphoreType.DMA
     return pl.pallas_call(
         basis_project_kernel,
-        out_shape=(jax.ShapeDtypeStruct((GX * ycount, RANK // GX, BLOCK), jnp.float32),
+        out_shape=(jax.ShapeDtypeStruct((RANK // GX, GX * ycount, BLOCK), jnp.float32),
                    jax.ShapeDtypeStruct((NX // GX, RANK), jnp.float32)),
         in_specs=[pl.BlockSpec(memory_space=VMEM)] * 2 + [pl.BlockSpec(memory_space=pl.ANY)],
         out_specs=(pl.BlockSpec(memory_space=VMEM),) * 2,
@@ -388,8 +374,8 @@
 
 def local(snapshot):
     fib, early, late = gather_gram(snapshot)
-    returned, mine = basis_project(fib, early, late)
-    return (mine, jnp.transpose(returned, (1, 0, 2)))
+    core, mine = basis_project(fib, early, late)
+    return (mine, core)
 
 
 def solution(mesh):

time: 147 us -> 141 us (0.959)
  Pallas kernels: 143 us -> 136 us
    pallas_call x1, Pallas kernels: 106 us -> 100 us  [gather_gram(): pl.pallas_call(gather_gram_kernel, out_shape=(jax.ShapeDtypeStruct((ycoun...]
where the time goes in v4:
time: 141 us; the launch traced here: 140 us
  Pallas kernels  136 us (96%)
  local copies, waits for them, and re-layouts  3.29 us (2%)
    pallas_call x1, Pallas kernels, gather_gram(): pl.pallas_call(gather_gram_kernel, out_shape=(jax.ShapeDtypeStruct((ycoun...  100 us
    pallas_call x1, Pallas kernels, basis_project(): pl.pallas_call(basis_project_kernel, out_shape=(jax.ShapeDtypeStruct((RAN...  36.3 us
    unnamed x2, local copies, waits for them, and re-layouts  3.29 us

profile of v4, /device:TPU:1, one launch (start us, length us, event | category | flops | bytes accessed | tf_op | source)
XLA Modules:
  0.0 140.4 jit_solution(8974300225366746377)
XLA Ops:
  0.6 100.2 %shard_map.30 = (f32[10,512,128]{2,1,0:T(8,128)}, f32[1024,128]{1,0:T(8,128)}, f32[512,128]{1,0:T(8,128)}) custom-call(f32[32,160,128]{2,1,0:T(8,128)} %snap_ref.1), custom_call_target="tpu_custom_call" | custom-call | tf_op jit(solution)/shard_map/pallas_call | solution.py:223
  100.8 36.3 %shard_map.31 = (f32[8,160,128]{2,1,0:T(8,128)}, f32[32,128]{1,0:T(8,128)}) custom-call(f32[1024,128]{1,0:T(8,128)} %get-tuple-element.7.early_ref, f32[512,128]{1,0:T(8,128)} %get-tuple-element.8.late_ref, f32[10,512,128]{2,1,0:T(8,128)} %get-tuple-element.9.fib_hbm), custom_call_target="tpu_custom_call" | custom-call | tf_op jit(solution)/shard_map/pallas_call | solution.py:360
  137.1 1.3 copy.5
  138.4 2.0 %copy.6 = f32[8,160,128]{2,1,0:T(8,128)} copy(f32[8,160,128]{2,1,0:T(8,128)} %get-tuple-element.15) | data formatting | bytes 1310720

commit v5 on v4

--- a/solution.py
+++ b/solution.py
@@ -17,7 +17,7 @@
 FIRST = EARLY * GX
 EARLY_PIECE, LATE_PIECE = 16, 8
 SPLIT = 5
-STEPS = 10
+STEPS = 12
 
 
 def split(x):
@@ -59,12 +59,15 @@
         self.slot = gy * GZ + gz
         self.mine = pl.multiple_of(self.core * self.rows, self.rows)
         self.other = pl.multiple_of((1 - self.core) * self.rows, self.rows)
-        self.plane = []
+        self.near, self.far = [], []
         for dy in range(GY):
             for dx in range(GZ):
-                if (dy, dx) != (0, 0):
+                hops = min(dy, GY - dy) + min(dx, GZ - dx)
+                if hops:
                     ty, tx = lax.rem(gy + dy, GY), lax.rem(gz + dx, GZ)
-                    self.plane.append((dy * GZ + dx - 1, ty * GZ + tx, {"gy": ty, "gz": tx}))
+                    side = self.near if hops <= 2 else self.far
+                    side.append((dy * GZ + dx - 1, ty * GZ + tx, {"gy": ty, "gz": tx}))
+        self.plane = self.far + self.near
         self.at = pl.ds(pl.multiple_of(self.mine + self.slot * piece, 8), piece)
 
     def copy(self, src, dst, step, device):
@@ -90,12 +93,16 @@
     def start_plane(self):
         self.swap().wait()
         self.half[...] += self.acc[pl.ds(self.mine, self.rows), :]
-        for n, theirs, device in self.plane:
-            src = self.half.at[pl.ds(pl.multiple_of(theirs * self.piece, 8), self.piece)]
-            self.copy(src, self.parts.at[n], 1, device).start()
+        for step, side in ((5, self.far), (1, self.near)):
+            for n, theirs, device in side:
+                src = self.half.at[pl.ds(pl.multiple_of(theirs * self.piece, 8), self.piece)]
+                self.copy(src, self.parts.at[n], step, device).start()
+
+    def near_arrived(self):
+        self.taken(1, len(self.near))
 
     def start_levels(self):
-        self.taken(1, PLANE - 1)
+        self.taken(5, len(self.far))
         total = self.half[pl.ds(pl.multiple_of(self.slot * self.piece, 8), self.piece), :]
         for n in range(PLANE - 1):
             total = total + self.parts[n]
@@ -189,6 +196,7 @@
     lax.fori_loop(0, SPLIT, take_early, 0)
     early.start_cores()
     early.start_plane()
+    early.near_arrived()
     early.start_levels()
 
     def take_late(g, carry):
@@ -198,8 +206,9 @@
     lax.fori_loop(0, SPLIT, take_late, 0)
     late.start_cores()
     late.start_plane()
+    late.near_arrived()
+    early.start_gather()
     late.start_levels()
-    early.start_gather()
     late.start_gather()
     early.start_back()
     late.start_back()
@@ -372,9 +381,24 @@
     )(early, late, fib)
 
 
+def finish_kernel(core_ref, mine_ref, core_out, mine_out):
+    core_out[...] = core_ref[...]
+    mine_out[...] = mine_ref[...]
+
+
+def finish(core, mine):
+    return pl.pallas_call(
+        finish_kernel,
+        out_shape=(jax.ShapeDtypeStruct(core.shape, core.dtype), jax.ShapeDtypeStruct(mine.shape, mine.dtype)),
+        in_specs=[pl.BlockSpec(memory_space=VMEM)] * 2,
+        out_specs=(pl.BlockSpec(memory_space=VMEM),) * 2,
+    )(core, mine)
+
+
 def local(snapshot):
     fib, early, late = gather_gram(snapshot)
     core, mine = basis_project(fib, early, late)
+    core, mine = finish(core, mine)
     return (mine, core)
 
 

time: 141 us -> 138 us (0.979)
  local copies, waits for them, and re-layouts: 3.29 us -> 0 us
    unnamed x2 -> x0, local copies, waits for them, and re-layouts: 3.29 us -> none
    pallas_call x0 -> x1, Pallas kernels: none -> 1.97 us  [finish(): pl.pallas_call(finish_kernel, out_shape=(jax.ShapeDtypeStruct(core.shape,...]
    pallas_call x1, Pallas kernels: 100 us -> 98.5 us  [gather_gram(): pl.pallas_call(gather_gram_kernel, out_shape=(jax.ShapeDtypeStruct((ycoun...]
where the time goes in v5:
time: 138 us
  Pallas kernels  137 us (99%)
    pallas_call x1, Pallas kernels, gather_gram(): pl.pallas_call(gather_gram_kernel, out_shape=(jax.ShapeDtypeStruct((ycoun...  98.5 us
    pallas_call x1, Pallas kernels, basis_project(): pl.pallas_call(basis_project_kernel, out_shape=(jax.ShapeDtypeStruct((RAN...  36.6 us

profile of v5, /device:TPU:1, one launch (start us, length us, event | category | flops | bytes accessed | tf_op | source)
XLA Modules:
  0.0 137.7 jit_solution(17034852377844237504)
XLA Ops:
  0.6 98.5 %shard_map.30 = (f32[10,512,128]{2,1,0:T(8,128)}, f32[1024,128]{1,0:T(8,128)}, f32[512,128]{1,0:T(8,128)}) custom-call(f32[32,160,128]{2,1,0:T(8,128)} %snap_ref.1), custom_call_target="tpu_custom_call" | custom-call | tf_op jit(solution)/shard_map/pallas_call | solution.py:232
  99.2 36.6 %shard_map.31 = (f32[8,160,128]{2,1,0:T(8,128)}, f32[32,128]{1,0:T(8,128)}) custom-call(f32[1024,128]{1,0:T(8,128)} %get-tuple-element.9.early_ref, f32[512,128]{1,0:T(8,128)} %get-tuple-element.10.late_ref, f32[10,512,128]{2,1,0:T(8,128)} %get-tuple-element.11.fib_hbm), custom_call_target="tpu_custom_call" | custom-call | tf_op jit(solution)/shard_map/pallas_call | solution.py:369
  135.8 2.0 %shard_map.32 = (f32[8,160,128]{2,1,0:T(8,128)}, f32[32,128]{1,0:T(8,128)}) custom-call(f32[8,160,128]{2,1,0:T(8,128)} %get-tuple-element.12.core_ref, f32[32,128]{1,0:T(8,128)} %get-tuple-element.13.mine_ref), custom_call_target="tpu_custom_call" | custom-call | tf_op jit(solution)/shard_map/pallas_call | solution.py:390

commit v6 on v5

--- a/solution.py
+++ b/solution.py
@@ -371,7 +371,7 @@
         out_shape=(jax.ShapeDtypeStruct((RANK // GX, GX * ycount, BLOCK), jnp.float32),
                    jax.ShapeDtypeStruct((NX // GX, RANK), jnp.float32)),
         in_specs=[pl.BlockSpec(memory_space=VMEM)] * 2 + [pl.BlockSpec(memory_space=pl.ANY)],
-        out_specs=(pl.BlockSpec(memory_space=VMEM),) * 2,
+        out_specs=(pl.BlockSpec(memory_space=pl.ANY), pl.BlockSpec(memory_space=VMEM)),
         scratch_shapes=[VMEM((ycount, NX, BLOCK), jnp.float32),
                         VMEM((NX, NX), jnp.bfloat16), VMEM((NX, NX), jnp.bfloat16),
                         VMEM((RANK, NX), jnp.float32), VMEM((RANK, NX), jnp.float32),

time: 138 us -> 138 us (level)
  no operation moved by 1% of the time
where the time goes in v6:
time: 138 us
  Pallas kernels  137 us (99%)
    pallas_call x1, Pallas kernels, gather_gram(): pl.pallas_call(gather_gram_kernel, out_shape=(jax.ShapeDtypeStruct((ycoun...  98.5 us
    pallas_call x1, Pallas kernels, basis_project(): pl.pallas_call(basis_project_kernel, out_shape=(jax.ShapeDtypeStruct((RAN...  36.4 us

profile of v6, /device:TPU:1, one launch (start us, length us, event | category | flops | bytes accessed | tf_op | source)
XLA Modules:
  0.0 137.6 jit_solution(109853788017186281)
XLA Ops:
  0.6 98.5 %shard_map.30 = (f32[10,512,128]{2,1,0:T(8,128)}, f32[1024,128]{1,0:T(8,128)}, f32[512,128]{1,0:T(8,128)}) custom-call(f32[32,160,128]{2,1,0:T(8,128)} %snap_ref.1), custom_call_target="tpu_custom_call" | custom-call | tf_op jit(solution)/shard_map/pallas_call | solution.py:232
  99.2 36.4 %shard_map.31 = (f32[8,160,128]{2,1,0:T(8,128)}, f32[32,128]{1,0:T(8,128)}) custom-call(f32[1024,128]{1,0:T(8,128)} %get-tuple-element.9.early_ref, f32[512,128]{1,0:T(8,128)} %get-tuple-element.10.late_ref, f32[10,512,128]{2,1,0:T(8,128)} %get-tuple-element.11.fib_hbm), custom_call_target="tpu_custom_call" | custom-call | tf_op jit(solution)/shard_map/pallas_call | solution.py:369
  135.6 2.0 %shard_map.32 = (f32[8,160,128]{2,1,0:T(8,128)}, f32[32,128]{1,0:T(8,128)}) custom-call(f32[8,160,128]{2,1,0:T(8,128)} %get-tuple-element.12.core_ref, f32[32,128]{1,0:T(8,128)} %get-tuple-element.13.mine_ref), custom_call_target="tpu_custom_call" | custom-call | tf_op jit(solution)/shard_map/pallas_call | solution.py:390
